TPU v7x, 32 devices: a whole 2x2x4 slice. The times are simulated.
32 devices in a mesh: lat: 4 (over y, core), lon: 8 (over z, x).
Axes of the slice: x: 2, y: 2, z: 4, core: 2. Of those that a mesh axis runs over, the one named last changes fastest.
Arguments:
- queries: bfloat16 [64, 128, 512], P('lat', 'lon'), may hold values from -6 to 6
- keys: bfloat16 [64, 128, 512], P('lat', 'lon'), may hold values from -6 to 6
- values: bfloat16 [64, 128, 512], P('lat', 'lon'), may hold values from -16 to 16
- rel_bias: float32 [8, 13, 13], replicated, may hold values from -4 to 4
- out_weight: bfloat16 [512, 1024], replicated, may hold values from -0.25 to 0.25
- cotangent: bfloat16 [64, 128, 1024], P('lat', 'lon'), may hold values from -16 to 16
Outputs:
- block_out: bfloat16 [64, 128, 1024], P('lat', 'lon')
- query_grad: bfloat16 [64, 128, 512], P('lat', 'lon')
- key_grad: bfloat16 [64, 128, 512], P('lat', 'lon')
- value_grad: bfloat16 [64, 128, 512], P('lat', 'lon')
- weight_grad: bfloat16 [512, 1024], replicated
- bias_grad: float32 [8, 13, 13], replicated
All inputs are finite; a program needn't handle non-finite values.
Results may differ from a plain program's by a relative error of at most 0.007.
Values may be sent and summed in bfloat16 or wider, within the bound.
No kernel may reach another device: no remote copies, remote signals or barrier semaphores. Data moves between devices by JAX's collectives and lax.ppermute only.
A program may use at most 128 MiB of HBM per device.

v0:
```python
import jax
import jax.numpy as jnp
from jax import lax
from jax.sharding import PartitionSpec as P

RAD = 6


def with_halo(block, sides, width, periodic):
    for axis, dim in sides:
        count = lax.axis_size(axis)
        forward = [(i, i + 1) for i in range(count - 1)]
        if periodic:
            forward.append((count - 1, 0))
        backward = [(target, source) for source, target in forward]
        low = lax.ppermute(
            lax.slice_in_dim(block, block.shape[dim] - width, None, axis=dim), axis, forward
        )
        high = lax.ppermute(lax.slice_in_dim(block, 0, width, axis=dim), axis, backward)
        block = jnp.concatenate([low, block, high], axis=dim)
    return block


def from_behind(block, axis, distance):
    devices = range(lax.axis_size(axis))
    route = [(i - distance, i) for i in devices if i - distance in devices]
    return lax.ppermute(block, axis, route)


def from_behind_2(value, axis, steps):
    count = lax.axis_size(axis)
    pairs = [(source, (source + steps) % count) for source in range(count)]
    return lax.ppermute(value, axis, pairs)


def relative_table(count_query, count_key):
    query_pos = jnp.arange(count_query, dtype=jnp.int32)
    key_pos = jnp.arange(count_key, dtype=jnp.int32)
    offset_pos = jnp.arange(2 * RAD + 1, dtype=jnp.int32)
    relative = key_pos[None, :] - query_pos[:, None]
    return (relative[:, :, None] == offset_pos[None, None, :]).astype(jnp.float32)


def shards(queries, keys, values, rel_bias, out_weight, cotangent):
    lat_dev, lon_dev, width = queries.shape
    heads = rel_bias.shape[0]
    head_size = width // heads
    outer_lat = lat_dev + 2 * RAD
    outer_lon = lon_dev + 2 * RAD
    count_query = lat_dev * lon_dev
    count_key = outer_lat * outer_lon
    tokens_all = count_query * lax.axis_size("lat") * lax.axis_size("lon")
    scale = head_size ** (-0.5)
    norm_factor = tokens_all ** (-0.5)
    paired = jnp.concatenate((keys, values), 2)
    widened = with_halo(paired, (("lon", 1),), RAD, True)
    outer = with_halo(widened, (("lat", 0),), RAD, False)
    outer_rows = outer.reshape(count_key, 2 * width)
    row_hot = relative_table(lat_dev, outer_lat)
    col_hot = relative_table(lon_dev, outer_lon)
    global_row = lax.axis_index("lat") * lat_dev + jnp.arange(outer_lat, dtype=jnp.int32) - RAD
    row_inside = ((global_row >= 0) & (global_row < lat_dev * lax.axis_size("lat"))).astype(
        jnp.float32
    )
    row_keep = row_hot * row_inside[None, :, None]
    bias_table = jnp.einsum(
        "hab,ika,jlb->hijkl", rel_bias, row_keep, col_hot, precision=lax.Precision.HIGHEST
    )
    keep_table = jnp.einsum("ika,jlb->ijkl", row_keep, col_hot, precision=lax.Precision.HIGHEST)
    keep_flat = keep_table.reshape(1, count_query, count_key) > 0.5
    masked_bias = jnp.where(keep_flat, bias_table.reshape(heads, count_query, count_key), -jnp.inf)
    query_heads = queries.reshape(count_query, heads, head_size).transpose(1, 0, 2)
    key_heads = outer_rows[:, :width].reshape(count_key, heads, head_size).transpose(1, 0, 2)
    value_heads = outer_rows[:, width:].reshape(count_key, heads, head_size).transpose(1, 0, 2)

    def weights_of(query_one, key_one, bias_one):
        scores = (
            lax.dot_general(
                query_one, key_one, (((1,), (1,)), ((), ())), preferred_element_type=jnp.float32
            )
            * scale
        )
        scores = scores + bias_one
        lifted = jnp.exp(scores - jnp.max(scores, -1, keepdims=True))
        return lifted / jnp.sum(lifted, -1, keepdims=True)

    def forward_head(items):
        query_one, key_one, value_one, bias_one = items
        probs = weights_of(query_one, key_one, bias_one)
        return jnp.dot(probs.astype(jnp.bfloat16), value_one, preferred_element_type=jnp.float32)

    mixed = lax.map(forward_head, (query_heads, key_heads, value_heads, masked_bias))
    attended = mixed.transpose(1, 0, 2).reshape(count_query, width).astype(jnp.bfloat16)
    block_out = jnp.dot(attended, out_weight, preferred_element_type=jnp.float32).astype(
        jnp.bfloat16
    )
    block_out = block_out.reshape(lat_dev, lon_dev, out_weight.shape[1])
    grad_rows = cotangent.reshape(count_query, cotangent.shape[2])
    attended_grad = lax.dot_general(
        grad_rows, out_weight, (((1,), (1,)), ((), ())), preferred_element_type=jnp.float32
    ).astype(jnp.bfloat16)
    weight_local = lax.dot_general(
        attended, grad_rows, (((0,), (0,)), ((), ())), preferred_element_type=jnp.float32
    )
    grad_heads = attended_grad.reshape(count_query, heads, head_size).transpose(1, 0, 2)

    def backward_head(items):
        query_one, key_one, value_one, grad_one, bias_one = items
        probs = weights_of(query_one, key_one, bias_one)
        rounded = probs.astype(jnp.bfloat16)
        slopes = lax.dot_general(
            grad_one, value_one, (((1,), (1,)), ((), ())), preferred_element_type=jnp.float32
        )
        inner_sum = jnp.sum(probs * slopes, -1, keepdims=True)
        score_grad = probs * (slopes - inner_sum)
        bias_part = jnp.einsum(
            "ijkl,ika,jlb->ab",
            score_grad.reshape(lat_dev, lon_dev, outer_lat, outer_lon),
            row_hot,
            col_hot,
            precision=lax.Precision.HIGHEST,
        )
        score_round = score_grad.astype(jnp.bfloat16)
        query_part = jnp.dot(score_round, key_one, preferred_element_type=jnp.float32) * scale
        key_part = (
            lax.dot_general(
                score_round, query_one, (((0,), (0,)), ((), ())), preferred_element_type=jnp.float32
            )
            * scale
        )
        value_part = lax.dot_general(
            rounded, grad_one, (((0,), (0,)), ((), ())), preferred_element_type=jnp.float32
        )
        return (query_part, key_part, value_part, bias_part)

    query_part, key_part, value_part, bias_local = lax.map(
        backward_head, (query_heads, key_heads, value_heads, grad_heads, masked_bias)
    )
    query_grad = query_part.transpose(1, 0, 2).reshape(lat_dev, lon_dev, width).astype(jnp.bfloat16)
    key_flat = key_part.transpose(1, 0, 2).reshape(count_key, width)
    value_flat = value_part.transpose(1, 0, 2).reshape(count_key, width)
    terms = jnp.concatenate((key_flat, value_flat), 1).reshape(outer_lat, outer_lon, 2 * width)
    top_rows = terms[:RAD]
    bottom_rows = terms[outer_lat - RAD :]
    middle = terms[RAD : RAD + lat_dev]
    from_below = from_behind(top_rows.astype(jnp.bfloat16), "lat", -1).astype(top_rows.dtype)
    from_above = from_behind(bottom_rows, "lat", 1)
    middle = middle.at[lat_dev - RAD :].add(from_below)
    middle = middle.at[:RAD].add(from_above)
    west_cols = middle[:, :RAD]
    east_cols = middle[:, outer_lon - RAD :]
    center = middle[:, RAD : RAD + lon_dev]
    from_east = from_behind_2(west_cols, "lon", -1)
    from_west = from_behind_2(east_cols, "lon", 1)
    center = center.at[:, lon_dev - RAD :].add(from_east)
    center = center.at[:, :RAD].add(from_west)
    key_grad = center[:, :, :width].astype(jnp.bfloat16)
    value_grad = center[:, :, width:].astype(jnp.bfloat16)
    weight_total, bias_total = lax.psum((weight_local, bias_local), ("lat", "lon"))
    weight_grad = (weight_total * norm_factor).astype(jnp.bfloat16)
    bias_grad = bias_total * norm_factor
    return (block_out, query_grad, key_grad, value_grad, weight_grad, bias_grad)


def solution(mesh):
    in_specs = (
        P("lat", "lon", None),
        P("lat", "lon", None),
        P("lat", "lon", None),
        P(),
        P(),
        P("lat", "lon", None),
    )
    out_specs = (
        P("lat", "lon", None),
        P("lat", "lon", None),
        P("lat", "lon", None),
        P("lat", "lon", None),
        P(),
        P(),
    )
    return jax.shard_map(shards, mesh=mesh, in_specs=in_specs, out_specs=out_specs, check_vma=False)
```

profile of v0, /device:TPU:0, one launch (start us, length us, event | category | flops | bytes accessed | tf_op | source)
XLA Modules:
  0.0 482.4 jit_solution(6144126483298326666)
XLA Ops:
  10.2 6.0 %collective-permute-start.1 = (bf16[16,6,1024]{2,1,0:T(8,128)(2,1)}, bf16[16,6,1024]{2,1,0:T(8,128)(2,1)S(1)}, u32[]{:S(2)}, u32[]{:S(2)}) collective-permute-start(bf16[16,6,1024]{2,1,0:T(8,128)(2,1)} %get-tuple-element.320), channel_id=1, source_target_pairs={{1,0},{2,1},{3,2},{4,3},{5,4},{6,5},{7,6},{0,7},{9,8},{10,9},{11,1... | collective-permute-start | bytes 589832 | tf_op jit(solution)/shard_map/ppermute | solution.py:19
  17.3 14.0 %convolution_bitcast_fusion.4 = f32[8,16,16,28,28]{4,3,2,0,1:T(8,128)S(1)} fusion(f32[16,28,8,13,1]{1,3,4,2,0:T(8,128)S(1)} %convolution_bitcast_fusion.5, s32[16,28]{1,0:T(8,128)S(1)} %iota_subtract_fusion), kind=kOutput, calls=%fused_computation.61 | convolution fusion | flops 250484416 | bytes 6610688 | tf_op jit(solution)/shard_map/hab,ika,jlb->hijkl/dot_general | solution.py:66
  31.3 13.2 %copy.37 = f32[8,16,16,28,28]{4,3,2,1,0:T(8,128)} copy(f32[8,16,16,28,28]{4,3,2,0,1:T(8,128)S(1)} %convolution_bitcast_fusion.4) | data formatting | bytes 12845056 | tf_op jit(solution)/shard_map/hab,ika,jlb->hijkl/transpose | solution.py:66
  44.6 28.1 %reshape.215 = f32[8,256,784]{2,1,0:T(8,128)} reshape(f32[8,16,16,28,28]{4,3,2,1,0:T(8,128)} %copy.37) | data formatting | bytes 12845056 | tf_op jit(solution)/shard_map/reshape | solution.py:71
  73.4 3.4 gt.20
  79.4 3.9 collective-permute-start.2
  83.3 6.6 %broadcast_select_fusion = f32[8,256,784]{2,1,0:T(8,128)} fusion(f32[8,256,784]{2,1,0:T(8,128)} %reshape.215, pred[256,784]{1,0:T(8,128)(4,1)S(1)} %gt.20), kind=kLoop, calls=%fused_computation.70 | loop fusion | flops 1605632 | bytes 13045760 | tf_op jit(solution)/shard_map/jit(_where)/select_n | solution.py:71
  91.1 8.2 %copy.41 = f32[8,256,784]{1,2,0:T(8,128)} copy(f32[8,256,784]{2,1,0:T(8,128)} %broadcast_select_fusion) | data formatting | bytes 12845056 | tf_op jit(solution)/shard_map/while | solution.py:92
  111.5 151.7 %while.34 = (s32[]{:T(128)}, bf16[8,256,64]{1,2,0:T(8,128)(2,1)S(1)}, f32[8,784,64]{1,2,0:T(8,128)}, f32[8,784,64]{1,2,0:T(8,128)}, f32[8,13,13]{2,0,1:T(8,128)S...) while((s32[]{:T(128)}, ...), condition=%wide.region_10.11_spmd.clone.clone, body=%wide.region_6.10_spmd.clone.clone.sunk | while | flops 164370688 | bytes 14238653 | solution.py:136
  119.8 6.0 %reshape.233 = f32[16,16,28,28]{3,2,1,0:T(8,128)} reshape(f32[256,784]{1,0:T(8,128)S(1)} %copy.64) | data formatting | bytes 1605632 | tf_op jit(solution)/shard_map/while/body/eval_jaxpr/reshape | solution.py:118
  125.8 4.3 convolution_bitcast_fusion.8
  138.7 6.0 %reshape.233 = f32[16,16,28,28]{3,2,1,0:T(8,128)} reshape(f32[256,784]{1,0:T(8,128)S(1)} %copy.64) | data formatting | bytes 1605632 | tf_op jit(solution)/shard_map/while/body/eval_jaxpr/reshape | solution.py:118
  144.8 4.3 convolution_bitcast_fusion.8
  157.7 6.0 %reshape.233 = f32[16,16,28,28]{3,2,1,0:T(8,128)} reshape(f32[256,784]{1,0:T(8,128)S(1)} %copy.64) | data formatting | bytes 1605632 | tf_op jit(solution)/shard_map/while/body/eval_jaxpr/reshape | solution.py:118
  163.7 4.3 convolution_bitcast_fusion.8
  176.7 6.0 %reshape.233 = f32[16,16,28,28]{3,2,1,0:T(8,128)} reshape(f32[256,784]{1,0:T(8,128)S(1)} %copy.64) | data formatting | bytes 1605632 | tf_op jit(solution)/shard_map/while/body/eval_jaxpr/reshape | solution.py:118
  182.7 4.3 convolution_bitcast_fusion.8
  195.6 6.0 %reshape.233 = f32[16,16,28,28]{3,2,1,0:T(8,128)} reshape(f32[256,784]{1,0:T(8,128)S(1)} %copy.64) | data formatting | bytes 1605632 | tf_op jit(solution)/shard_map/while/body/eval_jaxpr/reshape | solution.py:118
  201.7 4.3 convolution_bitcast_fusion.8
  214.6 6.0 %reshape.233 = f32[16,16,28,28]{3,2,1,0:T(8,128)} reshape(f32[256,784]{1,0:T(8,128)S(1)} %copy.64) | data formatting | bytes 1605632 | tf_op jit(solution)/shard_map/while/body/eval_jaxpr/reshape | solution.py:118
  220.6 4.3 convolution_bitcast_fusion.8
  233.5 6.0 %reshape.233 = f32[16,16,28,28]{3,2,1,0:T(8,128)} reshape(f32[256,784]{1,0:T(8,128)S(1)} %copy.64) | data formatting | bytes 1605632 | tf_op jit(solution)/shard_map/while/body/eval_jaxpr/reshape | solution.py:118
  239.6 4.3 convolution_bitcast_fusion.8
  252.5 6.0 %reshape.233 = f32[16,16,28,28]{3,2,1,0:T(8,128)} reshape(f32[256,784]{1,0:T(8,128)S(1)} %copy.64) | data formatting | bytes 1605632 | tf_op jit(solution)/shard_map/while/body/eval_jaxpr/reshape | solution.py:118
  258.5 4.3 convolution_bitcast_fusion.8
  271.5 28.9 %while.33 = (s32[]{:T(128)}, bf16[8,256,64]{1,2,0:T(8,128)(2,1)}, bf16[8,256,64]{2,1,0:T(8,128)(2,1)}, bf16[8,784,64]{2,1,0:T(8,128)(2,1)}, f32[8,256,784]{1,2,0...) while((s32[]{:T(128)}, bf16[8,256,64]{1,2,0:T(8,128)(2,1)}, bf16[8,256,64]{2,1,0:T(8,128)(2,1)}, ...), condition=%wide.region_5.6_spmd, body=%wide.region_2.5_spmd.sunk | while | flops 52985344 | bytes 3751509 | solution.py:92
  304.4 4.0 collective-permute-start.5
  317.6 41.1 %psum.15 = f32[8,13,13]{2,0,1:T(8,128)S(1)} all-reduce(f32[8,13,13]{2,0,1:T(8,128)S(1)} %get-tuple-element.181), channel_id=1, replica_groups=mesh['lat'=4,'lon'=8] {'lat','lon'}, use_global_device_ids=true, to_apply=%region_12.13 | all-reduce | flops 1352 | bytes 10816 | tf_op jit(solution)/shard_map/psum | solution.py:159
  363.7 3.3 collective-permute-start.6
  371.8 88.9 %all-reduce.2.cloned.1.call-done = f32[512,1024]{1,0:T(8,128)} async-done(((f32[512,1024]{1,0:T(8,128)}), f32[512,1024]{1,0:T(8,128)}) %all-reduce.2.cloned.1.call-update) | async-done | bytes 2097168 | tf_op jit(solution)/shard_map/psum | solution.py:159
  465.5 3.1 scatter-add.16
  469.9 3.5 scatter-add.19
  (197 shorter events, 157.4 us)
Async XLA Ops:
  7.2 92.1 %copy-start = (bf16[512,1024]{1,0:T(8,128)(2,1)S(1)}, bf16[512,1024]{1,0:T(8,128)(2,1)}, u32[]{:S(2)}) copy-start(bf16[512,1024]{1,0:T(8,128)(2,1)} %param.22) | copy-start | bytes 3145732
  7.2 9.0 %copy-start.10 = (f32[8,13,13]{2,0,1:T(8,128)S(1)}, f32[8,13,13]{2,0,1:T(8,128)}, u32[]{:S(2)}) copy-start(f32[8,13,13]{2,0,1:T(8,128)} %param.21) | copy-start | bytes 16228
  7.2 453.6 %all-reduce.2.cloned.1.call-start = ((), (), s32[]{:S(2)}) async-start(), calls=%async_computation | async-start | bytes 4194304 | tf_op jit(solution)/shard_map/psum | solution.py:159
  10.2 66.7 %collective-permute-start.1 = (bf16[16,6,1024]{2,1,0:T(8,128)(2,1)}, bf16[16,6,1024]{2,1,0:T(8,128)(2,1)S(1)}, u32[]{:S(2)}, u32[]{:S(2)}) collective-permute-start(bf16[16,6,1024]{2,1,0:T(8,128)(2,1)} %get-tuple-element.320), channel_id=1, source_target_pairs={{1,0},{2,1},{3,2},{4,3},{5,4},{6,5},{7,6},{0,7},{9,8},{10,9},{11,1... | collective-permute-start | bytes 589832 | tf_op jit(solution)/shard_map/ppermute | solution.py:19
  16.1 60.7 %collective-permute-start = (bf16[16,6,1024]{2,1,0:T(8,128)(2,1)}, bf16[16,6,1024]{2,1,0:T(8,128)(2,1)S(1)}, u32[]{:S(2)}, u32[]{:S(2)}) collective-permute-start(bf16[16,6,1024]{2,1,0:T(8,128)(2,1)} %get-tuple-element.319), channel_id=1, source_target_pairs={{0,1},{1,2},{2,3},{3,4},{4,5},{5,6},{6,7},{7,0},{8,9},{9,10},{10,1... | collective-permute-start | bytes 589832 | tf_op jit(solution)/shard_map/ppermute | solution.py:16
  76.8 13.1 %copy-start.5 = (bf16[16,6,1024]{2,1,0:T(8,128)(2,1)}, bf16[16,6,1024]{2,1,0:T(8,128)(2,1)S(1)}, u32[]{:S(2)}) copy-start(bf16[16,6,1024]{2,1,0:T(8,128)(2,1)S(1)} %collective-permute-done.1) | copy-start | bytes 589828
  76.9 13.0 %copy-start.6 = (bf16[16,6,1024]{2,1,0:T(8,128)(2,1)}, bf16[16,6,1024]{2,1,0:T(8,128)(2,1)S(1)}, u32[]{:S(2)}) copy-start(bf16[16,6,1024]{2,1,0:T(8,128)(2,1)S(1)} %collective-permute-done) | copy-start | bytes 589828
  78.1 22.5 %collective-permute-start.3 = (bf16[6,28,1024]{2,1,0:T(8,128)(2,1)}, bf16[6,28,1024]{2,1,0:T(8,128)(2,1)}, u32[]{:S(2)}, u32[]{:S(2)}) collective-permute-start(bf16[6,28,1024]{2,1,0:T(8,128)(2,1)} %get-tuple-element.316), channel_id=1, source_target_pairs={{8,0},{16,8},{24,16},{9,1},{17,9},{25,17},{10,2},{18,10},{26,18},{... | collective-permute-start | bytes 1032200 | tf_op jit(solution)/shard_map/ppermute | solution.py:19
  79.4 10.5 %copy-start.9 = (bf16[16,16,512]{2,1,0:T(8,128)(2,1)S(1)}, bf16[16,16,512]{2,1,0:T(8,128)(2,1)}, u32[]{:S(2)}) copy-start(bf16[16,16,512]{2,1,0:T(8,128)(2,1)} %param.18) | copy-start | bytes 786436
  79.4 21.2 %collective-permute-start.2 = (bf16[6,28,1024]{2,1,0:T(8,128)(2,1)}, bf16[6,28,1024]{2,1,0:T(8,128)(2,1)}, u32[]{:S(2)}, u32[]{:S(2)}) collective-permute-start(bf16[6,28,1024]{2,1,0:T(8,128)(2,1)} %get-tuple-element.315), channel_id=1, source_target_pairs={{0,8},{8,16},{16,24},{1,9},{9,17},{17,25},{2,10},{10,18},{18,26},{... | collective-permute-start | bytes 1032200 | tf_op jit(solution)/shard_map/ppermute | solution.py:16
  91.1 8.2 %copy-start.4 = (bf16[16,16,1024]{2,1,0:T(8,128)(2,1)S(1)}, bf16[16,16,1024]{2,1,0:T(8,128)(2,1)}, u32[]{:S(2)}) copy-start(bf16[16,16,1024]{2,1,0:T(8,128)(2,1)} %param.23) | copy-start | bytes 1572868
  263.2 1.9 copy-start.7
  267.8 2.2 copy-start.1
  302.2 57.9 %collective-permute-start.4 = (bf16[6,28,1024]{2,1,0:T(8,128)(2,1)}, bf16[6,28,1024]{2,1,0:T(8,128)(2,1)}, u32[]{:S(2)}, u32[]{:S(2)}) collective-permute-start(bf16[6,28,1024]{2,1,0:T(8,128)(2,1)} %convert_element_type.74), channel_id=1, source_target_pairs={{8,0},{16,8},{24,16},{9,1},{17,9},{25,17},{10,2},{18,10},{26,18},{... | collective-permute-start | bytes 1032200 | tf_op jit(solution)/shard_map/ppermute | solution.py:27
  304.4 56.7 %collective-permute-start.5 = (f32[6,28,1024]{2,1,0:T(8,128)}, f32[6,28,1024]{2,1,0:T(8,128)}, u32[]{:S(2)}, u32[]{:S(2)}) collective-permute-start(f32[6,28,1024]{2,1,0:T(8,128)} %slice.163), channel_id=1, source_target_pairs={{0,8},{8,16},{16,24},{1,9},{9,17},{17,25},{2,10},{10,18},{18,26},{... | collective-permute-start | bytes 2064392 | tf_op jit(solution)/shard_map/ppermute | solution.py:27
  315.5 43.3 %copy-start.3 = (bf16[8,256,64]{1,2,0:T(8,128)(2,1)S(1)}, bf16[8,256,64]{1,2,0:T(8,128)(2,1)}, u32[]{:S(2)}) copy-start(bf16[8,256,64]{1,2,0:T(8,128)(2,1)} %get-tuple-element.177) | copy-start | bytes 786436
  358.8 1.3 copy-start.2
  361.1 6.5 %copy-start.8 = (bf16[8,256,64]{1,2,0:T(8,128)(2,1)S(1)}, bf16[8,256,64]{1,2,0:T(8,128)(2,1)}, u32[]{:S(2)}) copy-start(bf16[8,256,64]{1,2,0:T(8,128)(2,1)} %copy-done.7) | copy-start | bytes 786436
  363.7 99.9 %collective-permute-start.6 = (f32[16,6,1024]{2,1,0:T(8,128)}, f32[16,6,1024]{2,1,0:T(8,128)}, u32[]{:S(2)}, u32[]{:S(2)}) collective-permute-start(f32[16,6,1024]{2,1,0:T(8,128)} %get-tuple-element.312), channel_id=1, source_target_pairs={{0,7},{1,0},{2,1},{3,2},{4,3},{5,4},{6,5},{7,6},{8,15},{9,8},{10,9... | collective-permute-start | bytes 1179656 | tf_op jit(solution)/shard_map/ppermute | solution.py:33
  371.8 96.8 %collective-permute-start.7 = (f32[16,6,1024]{2,1,0:T(8,128)}, f32[16,6,1024]{2,1,0:T(8,128)}, u32[]{:S(2)}, u32[]{:S(2)}) collective-permute-start(f32[16,6,1024]{2,1,0:T(8,128)} %get-tuple-element.311), channel_id=1, source_target_pairs={{0,1},{1,2},{2,3},{3,4},{4,5},{5,6},{6,7},{7,0},{8,9},{9,10},{10,1... | collective-permute-start | bytes 1179656 | tf_op jit(solution)/shard_map/ppermute | solution.py:33
Sparse Core Ops, SparseCore 0:
  317.8 142.9 all-reduce.1
where the time goes:
time: 486 us; the launch traced here: 482 us
  matrix products  144 us (30%)
  local copies, waits for them, and re-layouts  143 us (29%)
  waiting for transfers between devices  89 us (18%)
  blocking collectives  41.1 us (8%)
  other arithmetic  30.6 us (6%)
  starting transfers between devices  19.8 us (4%)
  between operations  14.3 us (3%)
    psum x1, waiting for transfers between devices, shards(): lax.psum((weight_local, bias_local), ('lat', 'lon'))  88.9 us
    reshape x8, local copies, waits for them, and re-layouts, backward_head(): score_grad.reshape(lat_dev, lon_dev, outer_lat, outer_lon)  48.2 us
    psum x1, blocking collectives, shards(): lax.psum((weight_local, bias_local), ('lat', 'lon'))  41.1 us
    dot_general x16, matrix products, backward_head(): jnp.einsum('ijkl,ika,jlb->ab', score_grad.reshape(lat_dev, lon_dev, outer...  36.5 us
    reshape x1, local copies, waits for them, and re-layouts, shards(): bias_table.reshape(heads, count_query, count_key)  28.1 us
    dot_general x16, matrix products, weights_of(): lax.dot_general(query_one, key_one, (((1,), (1,)), ((), ())), preferred_e...  25.5 us
    dot_general x2, matrix products, shards(): jnp.einsum('hab,ika,jlb->hijkl', rel_bias, row_keep, col_hot, precision=l...  15 us
    dot_general x8, matrix products, forward_head(): jnp.dot(probs.astype(jnp.bfloat16), value_one, preferred_element_type=jnp...  14.7 us
  transfers between devices with their start and end apart: 9, of which 1 were waited for; matrix products, arithmetic and copies ran while one was open for 22% of the time, Pallas kernels for 0%

commit v1 on v0

--- a/solution.py
+++ b/solution.py
@@ -156,7 +156,7 @@
     center = center.at[:, :RAD].add(from_west)
     key_grad = center[:, :, :width].astype(jnp.bfloat16)
     value_grad = center[:, :, width:].astype(jnp.bfloat16)
-    weight_total, bias_total = lax.psum((weight_local, bias_local), ("lat", "lon"))
+    weight_total, bias_total = lax.psum(lax.psum((weight_local, bias_local), "lon"), "lat")
     weight_grad = (weight_total * norm_factor).astype(jnp.bfloat16)
     bias_grad = bias_total * norm_factor
     return (block_out, query_grad, key_grad, value_grad, weight_grad, bias_grad)

time: 486 us -> 424 us (0.87)
  waiting for transfers between devices: 89 us -> 10.6 us
  local copies, waits for them, and re-layouts: 143 us -> 154 us
  blocking collectives: 41.1 us -> 48.7 us
    psum x1 -> x2, waiting for transfers between devices: 88.9 us -> 0.01 us  [the longest x1 0.01 us: shards(): lax.psum((weight_local, bias_local), 'lon')]
    dynamic_update_slice x16, local copies, waits for them, and re-layouts: 0.85 us -> 12.2 us  [shards(): lax.map(backward_head, (query_heads, key_heads, value_heads, grad_heads,...]
    ppermute x2, waiting for transfers between devices: 0.01 us -> 10.5 us  [from_behind_2(): return lax.ppermute(value, axis, pairs)]
    psum x1 -> x2, blocking collectives: 41.1 us -> 48.7 us  [the longest x1 37.1 us: shards(): lax.psum((weight_local, bias_local), 'lon')]
    dot_general x8, matrix products: 14.7 us -> 9.74 us  [forward_head(): jnp.dot(probs.astype(jnp.bfloat16), value_one, preferred_element_type=jnp...]
  transfers between devices with their start and end apart: 9 -> 10, of which waited for: 1 -> 1; matrix products, arithmetic and copies ran while one was open for 22% -> 67% of each run, Pallas kernels for 0% -> 0%
where the time goes in v1:
time: 424 us; the launch traced here: 420 us
  local copies, waits for them, and re-layouts  154 us (36%)
  matrix products  140 us (33%)
  blocking collectives  48.7 us (11%)
  other arithmetic  30.8 us (7%)
  starting transfers between devices  20.7 us (5%)
  between operations  14.4 us (3%)
  waiting for transfers between devices  10.6 us (2%)
    reshape x8, local copies, waits for them, and re-layouts, backward_head(): score_grad.reshape(lat_dev, lon_dev, outer_lat, outer_lon)  48.2 us
    dot_general x16, matrix products, backward_head(): jnp.einsum('ijkl,ika,jlb->ab', score_grad.reshape(lat_dev, lon_dev, outer...  37.7 us
    psum x1, blocking collectives, shards(): lax.psum((weight_local, bias_local), 'lon')  37.1 us
    dot_general x16, matrix products, weights_of(): lax.dot_general(query_one, key_one, (((1,), (1,)), ((), ())), preferred_e...  28.5 us
    reshape x1, local copies, waits for them, and re-layouts, shards(): bias_table.reshape(heads, count_query, count_key)  28.1 us
    dot_general x2, matrix products, shards(): jnp.einsum('hab,ika,jlb->hijkl', rel_bias, row_keep, col_hot, precision=l...  15 us
    dot_general x8, matrix products, backward_head(): lax.dot_general(score_round, query_one, (((0,), (0,)), ((), ())), preferr...  14.5 us
    dot_general x8, matrix products, backward_head(): lax.dot_general(rounded, grad_one, (((0,), (0,)), ((), ())), preferred_el...  13.9 us
  transfers between devices with their start and end apart: 10, of which 1 were waited for; matrix products, arithmetic and copies ran while one was open for 67% of the time, Pallas kernels for 0%

profile of v1, /device:TPU:0, one launch (start us, length us, event | category | flops | bytes accessed | tf_op | source)
XLA Modules:
  0.0 419.7 jit_solution(6959912537225461335)
XLA Ops:
  10.2 6.0 %collective-permute-start.1 = (bf16[16,6,1024]{2,1,0:T(8,128)(2,1)}, bf16[16,6,1024]{2,1,0:T(8,128)(2,1)S(1)}, u32[]{:S(2)}, u32[]{:S(2)}) collective-permute-start(bf16[16,6,1024]{2,1,0:T(8,128)(2,1)} %get-tuple-element.320), channel_id=1, source_target_pairs={{1,0},{2,1},{3,2},{4,3},{5,4},{6,5},{7,6},{0,7},{9,8},{10,9},{11,1... | collective-permute-start | bytes 589832 | tf_op jit(solution)/shard_map/ppermute | solution.py:19
  17.3 14.0 %convolution_bitcast_fusion.4 = f32[8,16,16,28,28]{4,3,2,0,1:T(8,128)S(1)} fusion(f32[16,28,8,13,1]{1,3,4,2,0:T(8,128)S(1)} %convolution_bitcast_fusion.5, s32[16,28]{1,0:T(8,128)S(1)} %iota_subtract_fusion), kind=kOutput, calls=%fused_computation.61 | convolution fusion | flops 250484416 | bytes 6610688 | tf_op jit(solution)/shard_map/hab,ika,jlb->hijkl/dot_general | solution.py:66
  31.3 13.2 %copy.37 = f32[8,16,16,28,28]{4,3,2,1,0:T(8,128)} copy(f32[8,16,16,28,28]{4,3,2,0,1:T(8,128)S(1)} %convolution_bitcast_fusion.4) | data formatting | bytes 12845056 | tf_op jit(solution)/shard_map/hab,ika,jlb->hijkl/transpose | solution.py:66
  44.6 28.1 %reshape.215 = f32[8,256,784]{2,1,0:T(8,128)} reshape(f32[8,16,16,28,28]{4,3,2,1,0:T(8,128)} %copy.37) | data formatting | bytes 12845056 | tf_op jit(solution)/shard_map/reshape | solution.py:71
  73.5 3.4 gt.20
  79.4 3.9 collective-permute-start.2
  83.4 6.6 %broadcast_select_fusion = f32[8,256,784]{2,1,0:T(8,128)} fusion(f32[8,256,784]{2,1,0:T(8,128)} %reshape.215, pred[256,784]{1,0:T(8,128)(4,1)S(1)} %gt.20), kind=kLoop, calls=%fused_computation.70 | loop fusion | flops 1605632 | bytes 13045760 | tf_op jit(solution)/shard_map/jit(_where)/select_n | solution.py:71
  91.1 8.2 %copy.41 = f32[8,256,784]{1,2,0:T(8,128)} copy(f32[8,256,784]{2,1,0:T(8,128)} %broadcast_select_fusion) | data formatting | bytes 12845056 | tf_op jit(solution)/shard_map/while | solution.py:92
  112.3 23.3 %while.33 = (s32[]{:T(128)}, bf16[8,256,64]{1,2,0:T(8,128)(2,1)S(1)}, bf16[8,256,64]{2,1,0:T(8,128)(2,1)}, bf16[8,784,64]{2,1,0:T(8,128)(2,1)S(1)}, f32[8,256,78...) while((s32[]{:T(128)}, bf16[8,256,64]{1,2,0:T(8,128)(2,1)S(1)}, bf16[8,256,64]{2,1,0:T(8,128)(2,1)}, ...), condition=%wide.region_5.6_spmd, body=%wide.region_2.5_spmd.sunk | while | flops 52985344 | bytes 3751509 | solution.py:92
  138.2 165.4 %while.34 = (s32[]{:T(128)}, bf16[8,256,64]{1,2,0:T(8,128)(2,1)}, f32[8,784,64]{1,2,0:T(8,128)}, f32[8,784,64]{1,2,0:T(8,128)}, f32[8,13,13]{2,0,1:T(8,128)}, /*...) while((s32[]{:T(128)}, bf16[8,256,64]{1,2,0:T(8,128)(2,1)}, ...), condition=%wide.region_10.11_spmd.clone.clone, body=%wide.region_6.10_spmd.clone.clone.sunk | while | flops 164370688 | bytes 20661236 | solution.py:136
  146.6 6.0 %reshape.233 = f32[16,16,28,28]{3,2,1,0:T(8,128)} reshape(f32[256,784]{1,0:T(8,128)S(1)} %copy.64) | data formatting | bytes 1605632 | tf_op jit(solution)/shard_map/while/body/eval_jaxpr/reshape | solution.py:118
  152.6 4.4 %convolution_bitcast_fusion.8 = f32[13,16,28]{2,0,1:T(8,128)S(1)} fusion(f32[16,16,28,28]{3,2,1,0:T(8,128)} %reshape.233, s32[16,28]{1,0:T(8,128)S(1)} %get-tuple-element.494), kind=kOutput, calls=%fused_computation.23.clone.1 | convolution fusion | flops 31321472 | bytes 827904 | tf_op jit(solution)/shard_map/while/body/eval_jaxpr/ijkl,ika,jlb->ab/dot_general | solution.py:116
  167.3 6.0 %reshape.233 = f32[16,16,28,28]{3,2,1,0:T(8,128)} reshape(f32[256,784]{1,0:T(8,128)S(1)} %copy.64) | data formatting | bytes 1605632 | tf_op jit(solution)/shard_map/while/body/eval_jaxpr/reshape | solution.py:118
  173.3 4.4 %convolution_bitcast_fusion.8 = f32[13,16,28]{2,0,1:T(8,128)S(1)} fusion(f32[16,16,28,28]{3,2,1,0:T(8,128)} %reshape.233, s32[16,28]{1,0:T(8,128)S(1)} %get-tuple-element.494), kind=kOutput, calls=%fused_computation.23.clone.1 | convolution fusion | flops 31321472 | bytes 827904 | tf_op jit(solution)/shard_map/while/body/eval_jaxpr/ijkl,ika,jlb->ab/dot_general | solution.py:116
  187.9 6.0 %reshape.233 = f32[16,16,28,28]{3,2,1,0:T(8,128)} reshape(f32[256,784]{1,0:T(8,128)S(1)} %copy.64) | data formatting | bytes 1605632 | tf_op jit(solution)/shard_map/while/body/eval_jaxpr/reshape | solution.py:118
  194.0 4.5 %convolution_bitcast_fusion.8 = f32[13,16,28]{2,0,1:T(8,128)S(1)} fusion(f32[16,16,28,28]{3,2,1,0:T(8,128)} %reshape.233, s32[16,28]{1,0:T(8,128)S(1)} %get-tuple-element.494), kind=kOutput, calls=%fused_computation.23.clone.1 | convolution fusion | flops 31321472 | bytes 827904 | tf_op jit(solution)/shard_map/while/body/eval_jaxpr/ijkl,ika,jlb->ab/dot_general | solution.py:116
  208.6 6.0 %reshape.233 = f32[16,16,28,28]{3,2,1,0:T(8,128)} reshape(f32[256,784]{1,0:T(8,128)S(1)} %copy.64) | data formatting | bytes 1605632 | tf_op jit(solution)/shard_map/while/body/eval_jaxpr/reshape | solution.py:118
  214.6 4.6 %convolution_bitcast_fusion.8 = f32[13,16,28]{2,0,1:T(8,128)S(1)} fusion(f32[16,16,28,28]{3,2,1,0:T(8,128)} %reshape.233, s32[16,28]{1,0:T(8,128)S(1)} %get-tuple-element.494), kind=kOutput, calls=%fused_computation.23.clone.1 | convolution fusion | flops 31321472 | bytes 827904 | tf_op jit(solution)/shard_map/while/body/eval_jaxpr/ijkl,ika,jlb->ab/dot_general | solution.py:116
  229.4 6.0 %reshape.233 = f32[16,16,28,28]{3,2,1,0:T(8,128)} reshape(f32[256,784]{1,0:T(8,128)S(1)} %copy.64) | data formatting | bytes 1605632 | tf_op jit(solution)/shard_map/while/body/eval_jaxpr/reshape | solution.py:118
  235.4 4.4 %convolution_bitcast_fusion.8 = f32[13,16,28]{2,0,1:T(8,128)S(1)} fusion(f32[16,16,28,28]{3,2,1,0:T(8,128)} %reshape.233, s32[16,28]{1,0:T(8,128)S(1)} %get-tuple-element.494), kind=kOutput, calls=%fused_computation.23.clone.1 | convolution fusion | flops 31321472 | bytes 827904 | tf_op jit(solution)/shard_map/while/body/eval_jaxpr/ijkl,ika,jlb->ab/dot_general | solution.py:116
  250.0 6.0 %reshape.233 = f32[16,16,28,28]{3,2,1,0:T(8,128)} reshape(f32[256,784]{1,0:T(8,128)S(1)} %copy.64) | data formatting | bytes 1605632 | tf_op jit(solution)/shard_map/while/body/eval_jaxpr/reshape | solution.py:118
  256.1 4.4 %convolution_bitcast_fusion.8 = f32[13,16,28]{2,0,1:T(8,128)S(1)} fusion(f32[16,16,28,28]{3,2,1,0:T(8,128)} %reshape.233, s32[16,28]{1,0:T(8,128)S(1)} %get-tuple-element.494), kind=kOutput, calls=%fused_computation.23.clone.1 | convolution fusion | flops 31321472 | bytes 827904 | tf_op jit(solution)/shard_map/while/body/eval_jaxpr/ijkl,ika,jlb->ab/dot_general | solution.py:116
  270.7 6.0 %reshape.233 = f32[16,16,28,28]{3,2,1,0:T(8,128)} reshape(f32[256,784]{1,0:T(8,128)S(1)} %copy.64) | data formatting | bytes 1605632 | tf_op jit(solution)/shard_map/while/body/eval_jaxpr/reshape | solution.py:118
  276.7 4.4 %convolution_bitcast_fusion.8 = f32[13,16,28]{2,0,1:T(8,128)S(1)} fusion(f32[16,16,28,28]{3,2,1,0:T(8,128)} %reshape.233, s32[16,28]{1,0:T(8,128)S(1)} %get-tuple-element.494), kind=kOutput, calls=%fused_computation.23.clone.1 | convolution fusion | flops 31321472 | bytes 827904 | tf_op jit(solution)/shard_map/while/body/eval_jaxpr/ijkl,ika,jlb->ab/dot_general | solution.py:116
  291.3 6.0 %reshape.233 = f32[16,16,28,28]{3,2,1,0:T(8,128)} reshape(f32[256,784]{1,0:T(8,128)S(1)} %copy.64) | data formatting | bytes 1605632 | tf_op jit(solution)/shard_map/while/body/eval_jaxpr/reshape | solution.py:118
  297.4 4.4 %convolution_bitcast_fusion.8 = f32[13,16,28]{2,0,1:T(8,128)S(1)} fusion(f32[16,16,28,28]{3,2,1,0:T(8,128)} %reshape.233, s32[16,28]{1,0:T(8,128)S(1)} %get-tuple-element.494), kind=kOutput, calls=%fused_computation.23.clone.1 | convolution fusion | flops 31321472 | bytes 827904 | tf_op jit(solution)/shard_map/while/body/eval_jaxpr/ijkl,ika,jlb->ab/dot_general | solution.py:116
  311.0 3.4 collective-permute-start.5
  326.8 4.7 %collective-permute-start.6 = (f32[16,6,1024]{2,1,0:T(8,128)}, f32[16,6,1024]{2,1,0:T(8,128)}, u32[]{:S(2)}, u32[]{:S(2)}) collective-permute-start(f32[16,6,1024]{2,1,0:T(8,128)} %get-tuple-element.312), channel_id=1, source_target_pairs={{0,7},{1,0},{2,1},{3,2},{4,3},{5,4},{6,5},{7,6},{8,15},{9,8},{10,9... | collective-permute-start | bytes 1179656 | tf_op jit(solution)/shard_map/ppermute | solution.py:33
  337.0 37.1 %psum.30 = f32[8,13,13]{2,0,1:T(8,128)S(1)} all-reduce(f32[8,13,13]{2,0,1:T(8,128)S(1)} %copy-done.11), channel_id=1, replica_groups=mesh['lat'=4,'lon'=8] {'lon'}, use_global_device_ids=true, to_apply=%region_13.14 | all-reduce | flops 1352 | bytes 10816 | tf_op jit(solution)/shard_map/psum | solution.py:159
  374.1 11.7 %psum.31 = f32[8,13,13]{2,0,1:T(8,128)S(1)} all-reduce(f32[8,13,13]{2,0,1:T(8,128)S(1)} %psum.30), channel_id=1, replica_groups=mesh['lat'=4,'lon'=8] {'lat'}, use_global_device_ids=true, to_apply=%region_14.15 | all-reduce | flops 1352 | bytes 10816 | tf_op jit(solution)/shard_map/psum | solution.py:159
  392.5 10.5 %collective-permute-done.7 = f32[16,6,1024]{2,1,0:T(8,128)} collective-permute-done((f32[16,6,1024]{2,1,0:T(8,128)}, f32[16,6,1024]{2,1,0:T(8,128)}, u32[]{:S(2)}, u32[]{:S(2)}) %collective-permute-start.7) | collective-permute-done | bytes 393248 | tf_op jit(solution)/shard_map/ppermute | solution.py:33
  404.3 3.5 scatter-add.19
  (231 shorter events, 166.6 us)
Async XLA Ops:
  7.2 92.2 %copy-start = (bf16[512,1024]{1,0:T(8,128)(2,1)S(1)}, bf16[512,1024]{1,0:T(8,128)(2,1)}, u32[]{:S(2)}) copy-start(bf16[512,1024]{1,0:T(8,128)(2,1)} %param.22) | copy-start | bytes 3145732
  7.2 9.0 %copy-start.10 = (f32[8,13,13]{2,0,1:T(8,128)S(1)}, f32[8,13,13]{2,0,1:T(8,128)}, u32[]{:S(2)}) copy-start(f32[8,13,13]{2,0,1:T(8,128)} %param.21) | copy-start | bytes 16228
  7.2 324.3 %all-reduce.3.cloned.1.call-start = ((), (), s32[]{:S(2)}) async-start(), calls=%async_computation | async-start | bytes 4194304 | tf_op jit(solution)/shard_map/psum | solution.py:159
  10.2 66.7 %collective-permute-start.1 = (bf16[16,6,1024]{2,1,0:T(8,128)(2,1)}, bf16[16,6,1024]{2,1,0:T(8,128)(2,1)S(1)}, u32[]{:S(2)}, u32[]{:S(2)}) collective-permute-start(bf16[16,6,1024]{2,1,0:T(8,128)(2,1)} %get-tuple-element.320), channel_id=1, source_target_pairs={{1,0},{2,1},{3,2},{4,3},{5,4},{6,5},{7,6},{0,7},{9,8},{10,9},{11,1... | collective-permute-start | bytes 589832 | tf_op jit(solution)/shard_map/ppermute | solution.py:19
  16.1 60.7 %collective-permute-start = (bf16[16,6,1024]{2,1,0:T(8,128)(2,1)}, bf16[16,6,1024]{2,1,0:T(8,128)(2,1)S(1)}, u32[]{:S(2)}, u32[]{:S(2)}) collective-permute-start(bf16[16,6,1024]{2,1,0:T(8,128)(2,1)} %get-tuple-element.319), channel_id=1, source_target_pairs={{0,1},{1,2},{2,3},{3,4},{4,5},{5,6},{6,7},{7,0},{8,9},{9,10},{10,1... | collective-permute-start | bytes 589832 | tf_op jit(solution)/shard_map/ppermute | solution.py:16
  76.9 13.1 %copy-start.7 = (bf16[16,6,1024]{2,1,0:T(8,128)(2,1)}, bf16[16,6,1024]{2,1,0:T(8,128)(2,1)S(1)}, u32[]{:S(2)}) copy-start(bf16[16,6,1024]{2,1,0:T(8,128)(2,1)S(1)} %collective-permute-done.1) | copy-start | bytes 589828
  76.9 13.1 %copy-start.8 = (bf16[16,6,1024]{2,1,0:T(8,128)(2,1)}, bf16[16,6,1024]{2,1,0:T(8,128)(2,1)S(1)}, u32[]{:S(2)}) copy-start(bf16[16,6,1024]{2,1,0:T(8,128)(2,1)S(1)} %collective-permute-done) | copy-start | bytes 589828
  78.1 22.5 %collective-permute-start.3 = (bf16[6,28,1024]{2,1,0:T(8,128)(2,1)}, bf16[6,28,1024]{2,1,0:T(8,128)(2,1)}, u32[]{:S(2)}, u32[]{:S(2)}) collective-permute-start(bf16[6,28,1024]{2,1,0:T(8,128)(2,1)} %get-tuple-element.316), channel_id=1, source_target_pairs={{8,0},{16,8},{24,16},{9,1},{17,9},{25,17},{10,2},{18,10},{26,18},{... | collective-permute-start | bytes 1032200 | tf_op jit(solution)/shard_map/ppermute | solution.py:19
  79.4 10.6 %copy-start.9 = (bf16[16,16,512]{2,1,0:T(8,128)(2,1)S(1)}, bf16[16,16,512]{2,1,0:T(8,128)(2,1)}, u32[]{:S(2)}) copy-start(bf16[16,16,512]{2,1,0:T(8,128)(2,1)} %param.18) | copy-start | bytes 786436
  79.4 21.2 %collective-permute-start.2 = (bf16[6,28,1024]{2,1,0:T(8,128)(2,1)}, bf16[6,28,1024]{2,1,0:T(8,128)(2,1)}, u32[]{:S(2)}, u32[]{:S(2)}) collective-permute-start(bf16[6,28,1024]{2,1,0:T(8,128)(2,1)} %get-tuple-element.315), channel_id=1, source_target_pairs={{0,8},{8,16},{16,24},{1,9},{9,17},{17,25},{2,10},{10,18},{18,26},{... | collective-permute-start | bytes 1032200 | tf_op jit(solution)/shard_map/ppermute | solution.py:16
  91.1 8.2 %copy-start.5 = (bf16[16,16,1024]{2,1,0:T(8,128)(2,1)S(1)}, bf16[16,16,1024]{2,1,0:T(8,128)(2,1)}, u32[]{:S(2)}) copy-start(bf16[16,16,1024]{2,1,0:T(8,128)(2,1)} %param.23) | copy-start | bytes 1572868
  112.3 23.4 %copy-start.6 = (bf16[16,16,1024]{2,1,0:T(8,128)(2,1)S(1)}, bf16[16,16,1024]{2,1,0:T(8,128)(2,1)}, u32[]{:S(2)}) copy-start(bf16[16,16,1024]{2,1,0:T(8,128)(2,1)} %param.23) | copy-start | bytes 1572868
  137.4 272.6 %all-reduce.5.cloned.1.call-start = ((), (), s32[]{:S(2)}) async-start(), calls=%async_computation.1 | async-start | bytes 4194304 | tf_op jit(solution)/shard_map/psum | solution.py:159
  138.2 3.7 copy-start.1
  152.6 6.2 %copy-start.2 = (bf16[8,784,64]{2,1,0:T(8,128)(2,1)S(1)}, bf16[8,784,64]{2,1,0:T(8,128)(2,1)}, u32[]{:S(2)}) copy-start(bf16[8,784,64]{2,1,0:T(8,128)(2,1)} %copy-done.1) | copy-start | bytes 2408452 | tf_op jit(solution)/shard_map/while
  158.9 3.7 copy-start.1
  173.3 6.2 %copy-start.2 = (bf16[8,784,64]{2,1,0:T(8,128)(2,1)S(1)}, bf16[8,784,64]{2,1,0:T(8,128)(2,1)}, u32[]{:S(2)}) copy-start(bf16[8,784,64]{2,1,0:T(8,128)(2,1)} %copy-done.1) | copy-start | bytes 2408452 | tf_op jit(solution)/shard_map/while
  179.5 3.7 copy-start.1
  194.0 6.3 %copy-start.2 = (bf16[8,784,64]{2,1,0:T(8,128)(2,1)S(1)}, bf16[8,784,64]{2,1,0:T(8,128)(2,1)}, u32[]{:S(2)}) copy-start(bf16[8,784,64]{2,1,0:T(8,128)(2,1)} %copy-done.1) | copy-start | bytes 2408452 | tf_op jit(solution)/shard_map/while
  214.6 6.4 %copy-start.2 = (bf16[8,784,64]{2,1,0:T(8,128)(2,1)S(1)}, bf16[8,784,64]{2,1,0:T(8,128)(2,1)}, u32[]{:S(2)}) copy-start(bf16[8,784,64]{2,1,0:T(8,128)(2,1)} %copy-done.1) | copy-start | bytes 2408452 | tf_op jit(solution)/shard_map/while
  221.0 3.7 copy-start.1
  235.4 6.2 %copy-start.2 = (bf16[8,784,64]{2,1,0:T(8,128)(2,1)S(1)}, bf16[8,784,64]{2,1,0:T(8,128)(2,1)}, u32[]{:S(2)}) copy-start(bf16[8,784,64]{2,1,0:T(8,128)(2,1)} %copy-done.1) | copy-start | bytes 2408452 | tf_op jit(solution)/shard_map/while
  256.1 6.2 %copy-start.2 = (bf16[8,784,64]{2,1,0:T(8,128)(2,1)S(1)}, bf16[8,784,64]{2,1,0:T(8,128)(2,1)}, u32[]{:S(2)}) copy-start(bf16[8,784,64]{2,1,0:T(8,128)(2,1)} %copy-done.1) | copy-start | bytes 2408452 | tf_op jit(solution)/shard_map/while
  276.7 6.2 %copy-start.2 = (bf16[8,784,64]{2,1,0:T(8,128)(2,1)S(1)}, bf16[8,784,64]{2,1,0:T(8,128)(2,1)}, u32[]{:S(2)}) copy-start(bf16[8,784,64]{2,1,0:T(8,128)(2,1)} %copy-done.1) | copy-start | bytes 2408452 | tf_op jit(solution)/shard_map/while
  282.9 3.7 copy-start.1
  297.4 6.2 %copy-start.2 = (bf16[8,784,64]{2,1,0:T(8,128)(2,1)S(1)}, bf16[8,784,64]{2,1,0:T(8,128)(2,1)}, u32[]{:S(2)}) copy-start(bf16[8,784,64]{2,1,0:T(8,128)(2,1)} %copy-done.1) | copy-start | bytes 2408452 | tf_op jit(solution)/shard_map/while
  311.0 13.3 %collective-permute-start.5 = (f32[6,28,1024]{2,1,0:T(8,128)}, f32[6,28,1024]{2,1,0:T(8,128)}, u32[]{:S(2)}, u32[]{:S(2)}) collective-permute-start(f32[6,28,1024]{2,1,0:T(8,128)} %slice.163), channel_id=1, source_target_pairs={{0,8},{8,16},{16,24},{1,9},{9,17},{17,25},{2,10},{10,18},{18,26},{... | collective-permute-start | bytes 2064392 | tf_op jit(solution)/shard_map/ppermute | solution.py:27
  315.5 7.5 %collective-permute-start.4 = (bf16[6,28,1024]{2,1,0:T(8,128)(2,1)S(1)}, bf16[6,28,1024]{2,1,0:T(8,128)(2,1)}, u32[]{:S(2)}, u32[]{:S(2)}) collective-permute-start(bf16[6,28,1024]{2,1,0:T(8,128)(2,1)S(1)} %convert_element_type.74), channel_id=1, source_target_pairs={{8,0},{16,8},{24,16},{9,1},{17,9},{25,17},{10,2},{18,10},{26,18},{... | collective-permute-start | bytes 1032200 | tf_op jit(solution)/shard_map/ppermute | solution.py:27
  325.7 5.9 %copy-start.4 = (bf16[8,256,64]{1,2,0:T(8,128)(2,1)S(1)}, bf16[8,256,64]{1,2,0:T(8,128)(2,1)}, u32[]{:S(2)}) copy-start(bf16[8,256,64]{1,2,0:T(8,128)(2,1)} %copy-done.3) | copy-start | bytes 786436
  326.8 60.8 %collective-permute-start.6 = (f32[16,6,1024]{2,1,0:T(8,128)}, f32[16,6,1024]{2,1,0:T(8,128)}, u32[]{:S(2)}, u32[]{:S(2)}) collective-permute-start(f32[16,6,1024]{2,1,0:T(8,128)} %get-tuple-element.312), channel_id=1, source_target_pairs={{0,7},{1,0},{2,1},{3,2},{4,3},{5,4},{6,5},{7,6},{8,15},{9,8},{10,9... | collective-permute-start | bytes 1179656 | tf_op jit(solution)/shard_map/ppermute | solution.py:33
  331.6 5.5 %copy-start.11 = (f32[8,13,13]{2,0,1:T(8,128)S(1)}, f32[8,13,13]{2,0,1:T(8,128)}, u32[]{:S(2)}) copy-start(f32[8,13,13]{2,0,1:T(8,128)} %get-tuple-element.181) | copy-start | bytes 16228
  385.8 17.3 %collective-permute-start.7 = (f32[16,6,1024]{2,1,0:T(8,128)}, f32[16,6,1024]{2,1,0:T(8,128)}, u32[]{:S(2)}, u32[]{:S(2)}) collective-permute-start(f32[16,6,1024]{2,1,0:T(8,128)} %get-tuple-element.311), channel_id=1, source_target_pairs={{0,1},{1,2},{2,3},{3,4},{4,5},{5,6},{6,7},{7,0},{8,9},{9,10},{10,1... | collective-permute-start | bytes 1179656 | tf_op jit(solution)/shard_map/ppermute | solution.py:33
  (4 other events, 12.8 us)
Sparse Core Ops, SparseCore 0:
  137.6 103.3 all-reduce.2
  331.7 50.2 all-reduce.4
